TPU v7x, 128 devices: a whole 4x4x4 slice. The times are simulated.
128 devices in a mesh: sector: 8 (over y, core), term: 16 (over x, z).
Axes of the slice: x: 4, y: 4, z: 4, core: 2. Of those that a mesh axis runs over, the one named last changes fastest.
Arguments:
- trial: float32 [16, 512, 512], P('sector', 'term'), may hold values from -6 to 6
- precond: float32 [16, 512, 512], P('sector', 'term'), may hold values from 2 to 16
- sector_dims: int32 [16], P('sector'), may hold values from 128 to 512
- left_ops: float32 [1024, 512, 512], P(('sector', 'term')), may hold values from -0.25 to 0.25
- right_ops: float32 [1024, 512, 512], P(('sector', 'term')), may hold values from -0.25 to 0.25
- task_source: int32 [1024], P(('sector', 'term')), may hold values from 0 to 1
- task_target: int32 [1024], P(('sector', 'term')), may hold values from 0 to 1
- task_count: int32 [128], P(('sector', 'term')), may hold values from 1 to 7, as said below
Outputs:
- trial_out: float32 [16, 512, 512], P('sector', 'term')
- ritz: float32 [3], replicated
Inputs may be any that keep to these rules, and one draw needn't show every extreme that they name: `task_count`: the counts of two devices with the same sector index whose term indices differ by half the term axis add up to 8.
All inputs are finite; a program needn't handle non-finite values.
Results may differ from a plain program's by a relative error of at most 0.0003.
Values sent between devices are 32-bit elements; how exact they have to be, the bound alone decides.
A program may use at most 64 MiB of HBM per device.

v0:
```python
import functools

import jax
import jax.numpy as jnp
from jax import lax
from jax.sharding import Mesh
from jax.sharding import PartitionSpec as P

STEPS = 3
SECTOR_TERM = ("sector_0", "sector_1", "term_0", "term_1")
SECTOR = ("sector_0", "sector_1")
TERM = ("term_0", "term_1")


def over_axes(shard, axes):
    return functools.reduce(lax.psum, axes, shard)


def from_everyone(shard, axis):
    copies = jnp.broadcast_to(shard, (lax.axis_size(axis), *shard.shape))
    return lax.all_to_all(copies, axis, split_axis=0, concat_axis=0, tiled=True)


def joined_along(tiles, dim):
    tiles = jnp.moveaxis(tiles, 0, dim)
    lengths = tiles.shape
    return tiles.reshape(*lengths[:dim], lengths[dim] * lengths[dim + 1], *lengths[dim + 2 :])


def gathered_copies(shard, axis, dim):
    tiles = from_everyone(shard, axis)
    return joined_along(tiles, dim)


def in_blocks(shard, dim, size):
    lengths = shard.shape
    tiles = shard.reshape(*lengths[:dim], size, lengths[dim] // size, *lengths[dim + 1 :])
    return jnp.moveaxis(tiles, dim, 0)


def summed_on_arrival(shard, axis, dim):
    size = lax.axis_size(axis)
    tiles = lax.all_to_all(in_blocks(shard, dim, size), axis, 0, 0, tiled=True)
    return jnp.sum(tiles, axis=0)


def apply_tasks(partial_value, full_vector, lefts, rights, sources, targets, first, last):
    highest = lax.Precision.HIGHEST

    def one(slot, total):
        block = lax.dynamic_index_in_dim(full_vector, sources[slot], 0, keepdims=False)
        inner = jnp.dot(block, rights[slot], precision=highest)
        product = jnp.dot(lefts[slot], inner, precision=highest)
        old = lax.dynamic_index_in_dim(total, targets[slot], 0, keepdims=True)
        return lax.dynamic_update_index_in_dim(total, old + product[None], targets[slot], 0)

    return lax.fori_loop(first, last, one, partial_value)


def rescale(vector, cells):
    total = over_axes(jnp.sum(vector * vector), SECTOR_TERM)
    return vector * jnp.sqrt(cells / total)


def per_device(
    trial, precond, sector_dims, left_ops, right_ops, task_source, task_target, task_count
):
    sec_dev, share, width = trial.shape
    cells = float(sec_dev * lax.axis_size(SECTOR) * width * width)
    start = lax.axis_index(TERM) * share
    rows = start + jnp.arange(share, dtype=jnp.int32)
    cols = jnp.arange(width, dtype=jnp.int32)
    limits = sector_dims[:, None]
    mask = ((rows[None, :] < limits)[:, :, None] & (cols[None, :] < limits)[:, None, :]).astype(
        jnp.float32
    )
    count = task_count[0]
    values = []
    vector = mask * trial
    for step in range(STEPS):
        full_vector = gathered_copies(vector, TERM, 1)
        partial_value = jnp.zeros((sec_dev, width, width), jnp.float32)
        partial_value = apply_tasks(
            partial_value, full_vector, left_ops, right_ops, task_source, task_target, 0, count
        )
        summed = summed_on_arrival(partial_value, TERM, 1)
        sig = summed * mask
        theta = over_axes(jnp.sum(vector * sig), SECTOR_TERM) / over_axes(
            jnp.sum(vector * vector), SECTOR_TERM
        )
        values.append(theta)
        vector = vector - (sig - theta * vector) / precond
    vector = rescale(vector, cells)
    return (vector, jnp.stack(values))


def solution(mesh):
    finer = Mesh(mesh.devices.reshape(4, 2, 4, 4), ("sector_0", "sector_1", "term_0", "term_1"))
    placed = (
        P(SECTOR, TERM, None),
        P(SECTOR, TERM, None),
        P(SECTOR),
        P(SECTOR_TERM, None, None),
        P(SECTOR_TERM, None, None),
        P(SECTOR_TERM),
        P(SECTOR_TERM),
        P(SECTOR_TERM),
    )
    return jax.shard_map(
        per_device,
        mesh=finer,
        in_specs=placed,
        out_specs=(P(SECTOR, TERM, None), P()),
        check_vma=False,
    )
```

profile of v0, /device:TPU:1, one launch (start us, length us, event | category | flops | bytes accessed | tf_op | source)
XLA Modules:
  0.0 587.6 jit_solution(16519058853156436209)
XLA Ops:
  4.7 8.4 %all-to-all-start = ((f32[16,2,32,512]{3,2,1,0:T(8,128)}), f32[16,2,32,512]{3,2,1,0:T(8,128)S(1)}, u32[]{:S(2)}, u32[]{:S(2)}) async-start(f32[16,2,32,512]{3,2,1,0:T(8,128)} %broadcast_in_dim.23), calls=%async_computation | async-start | bytes 4194304 | tf_op jit(solution)/shard_map/all_to_all | solution.py:21
  13.1 28.2 %all-to-all-done = f32[16,2,32,512]{3,2,1,0:T(8,128)S(1)} async-done(((f32[16,2,32,512]{3,2,1,0:T(8,128)}), f32[16,2,32,512]{3,2,1,0:T(8,128)S(1)}, u32[]{:S(2)}, u32[]{:S(2)}) %all-to-all-start) | async-done | bytes 2097184 | tf_op jit(solution)/shard_map/all_to_all | solution.py:21
  43.5 12.8 %while.30 = (s32[]{:T(128)}, f32[2,512,512]{2,1,0:T(8,128)S(1)}, s32[]{:T(128)}, s32[8]{0:T(128)S(1)}, f32[8,512,512]{2,1,0:T(8,128)}, /*index=5*/s32[8]{0:T(128...) while((s32[]{:T(128)}, f32[2,512,512]{2,1,0:T(8,128)S(1)}, ...), condition=%wide.region_1.2_spmd, body=%wide.region_0.1_spmd.sunk | while | flops 3221487616 | bytes 7340291 | solution.py:57
  46.7 3.4 fusion.58
  52.7 3.1 fusion.59
  56.6 100.3 %all_to_all.30 = f32[16,2,32,512]{3,2,1,0:T(8,128)S(1)} all-to-all(f32[16,2,32,512]{3,2,1,0:T(8,128)S(1)} %copy.11), channel_id=1, replica_groups=mesh['sector_0'=4,'sector_1'=2,'term_0'=4,'term_1'=4] {'term_0','term_1'}, dimensions={0} | all-to-all | bytes 4194304 | tf_op jit(solution)/shard_map/all_to_all | solution.py:43
  158.5 9.0 %all-reduce.8 = (f32[]{:T(128)}, f32[]{:T(128)}) all-reduce(f32[]{:T(128)} %get-tuple-element.139, f32[]{:T(128)} %get-tuple-element.138), channel_id=1, replica_groups=mesh['sector_0'=4,'sector_1'=2,'term_0'=4,'term_1'=4] {'sector_0'}, use_global_device_ids=true, to_apply=%region_4.5 | all-reduce | flops 2 | bytes 16 | tf_op jit(solution)/shard_map/psum | solution.py:16
  167.5 9.0 %all-reduce.11 = (f32[]{:T(128)}, f32[]{:T(128)}) all-reduce(f32[]{:T(128)} %get-tuple-element.204, f32[]{:T(128)} %get-tuple-element.205), channel_id=1, replica_groups=mesh['sector_0'=4,'sector_1'=2,'term_0'=4,'term_1'=4] {'sector_1'}, use_global_device_ids=true, to_apply=%region_5.6 | all-reduce | flops 2 | bytes 16 | tf_op jit(solution)/shard_map/psum | solution.py:16
  176.5 7.4 %all-reduce.5 = (f32[]{:T(128)}, f32[]{:T(128)}) all-reduce(f32[]{:T(128)} %get-tuple-element.210, f32[]{:T(128)} %get-tuple-element.211), channel_id=1, replica_groups=mesh['sector_0'=4,'sector_1'=2,'term_0'=4,'term_1'=4] {'term_0'}, use_global_device_ids=true, to_apply=%region_6.7 | all-reduce | flops 2 | bytes 16 | tf_op jit(solution)/shard_map/psum | solution.py:16
  184.0 7.0 %all-reduce.2 = (f32[]{:T(128)}, f32[]{:T(128)}) all-reduce(f32[]{:T(128)} %get-tuple-element.198, f32[]{:T(128)} %get-tuple-element.199), channel_id=1, replica_groups=mesh['sector_0'=4,'sector_1'=2,'term_0'=4,'term_1'=4] {'term_1'}, use_global_device_ids=true, to_apply=%region_7.8 | all-reduce | flops 2 | bytes 16 | tf_op jit(solution)/shard_map/psum | solution.py:16
  194.0 3.7 all-to-all-start.2
  197.7 24.5 %all-to-all-done.2 = f32[16,2,32,512]{3,2,1,0:T(8,128)S(1)} async-done(((f32[16,2,32,512]{3,2,1,0:T(8,128)}), f32[16,2,32,512]{3,2,1,0:T(8,128)S(1)}, u32[]{:S(2)}, u32[]{:S(2)}) %all-to-all-start.2) | async-done | bytes 2097184 | tf_op jit(solution)/shard_map/all_to_all | solution.py:21
  224.0 12.9 %while.31 = (s32[]{:T(128)}, f32[2,512,512]{2,1,0:T(8,128)S(1)}, s32[]{:T(128)}, s32[8]{0:T(128)S(1)}, f32[8,512,512]{2,1,0:T(8,128)}, /*index=5*/s32[8]{0:T(128...) while((s32[]{:T(128)}, f32[2,512,512]{2,1,0:T(8,128)S(1)}, ...), condition=%wide.region_14.15_spmd, body=%wide.region_13.14_spmd.sunk | while | flops 3221487616 | bytes 7340291 | solution.py:57
  227.2 3.4 fusion.64
  237.1 95.5 %all_to_all.31 = f32[16,2,32,512]{3,2,1,0:T(8,128)S(1)} all-to-all(f32[16,2,32,512]{3,2,1,0:T(8,128)S(1)} %copy.13), channel_id=1, replica_groups=mesh['sector_0'=4,'sector_1'=2,'term_0'=4,'term_1'=4] {'term_0','term_1'}, dimensions={0} | all-to-all | bytes 4194304 | tf_op jit(solution)/shard_map/all_to_all | solution.py:43
  333.5 15.0 %all-reduce.7 = (f32[]{:T(128)}, f32[]{:T(128)}) all-reduce(f32[]{:T(128)} %get-tuple-element.137, f32[]{:T(128)} %get-tuple-element.136), channel_id=1, replica_groups=mesh['sector_0'=4,'sector_1'=2,'term_0'=4,'term_1'=4] {'sector_0'}, use_global_device_ids=true, to_apply=%region_17.18 | all-reduce | flops 2 | bytes 16 | tf_op jit(solution)/shard_map/psum | solution.py:16
  348.6 9.4 %all-reduce.10 = (f32[]{:T(128)}, f32[]{:T(128)}) all-reduce(f32[]{:T(128)} %get-tuple-element.202, f32[]{:T(128)} %get-tuple-element.203), channel_id=1, replica_groups=mesh['sector_0'=4,'sector_1'=2,'term_0'=4,'term_1'=4] {'sector_1'}, use_global_device_ids=true, to_apply=%region_18.19 | all-reduce | flops 2 | bytes 16 | tf_op jit(solution)/shard_map/psum | solution.py:16
  358.0 7.4 %all-reduce.4 = (f32[]{:T(128)}, f32[]{:T(128)}) all-reduce(f32[]{:T(128)} %get-tuple-element.208, f32[]{:T(128)} %get-tuple-element.209), channel_id=1, replica_groups=mesh['sector_0'=4,'sector_1'=2,'term_0'=4,'term_1'=4] {'term_0'}, use_global_device_ids=true, to_apply=%region_19.20 | all-reduce | flops 2 | bytes 16 | tf_op jit(solution)/shard_map/psum | solution.py:16
  365.4 7.0 %all-reduce.1 = (f32[]{:T(128)}, f32[]{:T(128)}) all-reduce(f32[]{:T(128)} %get-tuple-element.196, f32[]{:T(128)} %get-tuple-element.197), channel_id=1, replica_groups=mesh['sector_0'=4,'sector_1'=2,'term_0'=4,'term_1'=4] {'term_1'}, use_global_device_ids=true, to_apply=%region_20.21 | all-reduce | flops 2 | bytes 16 | tf_op jit(solution)/shard_map/psum | solution.py:16
  375.4 3.9 all-to-all-start.4
  379.4 24.3 %all-to-all-done.4 = f32[16,2,32,512]{3,2,1,0:T(8,128)S(1)} async-done(((f32[16,2,32,512]{3,2,1,0:T(8,128)}), f32[16,2,32,512]{3,2,1,0:T(8,128)S(1)}, u32[]{:S(2)}, u32[]{:S(2)}) %all-to-all-start.4) | async-done | bytes 2097184 | tf_op jit(solution)/shard_map/all_to_all | solution.py:21
  405.5 12.9 %while.32 = (s32[]{:T(128)}, f32[2,512,512]{2,1,0:T(8,128)S(1)}, s32[]{:T(128)}, s32[8]{0:T(128)S(1)}, f32[8,512,512]{2,1,0:T(8,128)}, /*index=5*/s32[8]{0:T(128...) while((s32[]{:T(128)}, f32[2,512,512]{2,1,0:T(8,128)S(1)}, ...), condition=%wide.region_27.28_spmd, body=%wide.region_26.27_spmd.sunk | while | flops 3221487616 | bytes 7340291 | solution.py:57
  408.7 3.4 fusion.70
  418.6 95.5 %all_to_all.32 = f32[16,2,32,512]{3,2,1,0:T(8,128)S(1)} all-to-all(f32[16,2,32,512]{3,2,1,0:T(8,128)S(1)} %copy.15), channel_id=1, replica_groups=mesh['sector_0'=4,'sector_1'=2,'term_0'=4,'term_1'=4] {'term_0','term_1'}, dimensions={0} | all-to-all | bytes 4194304 | tf_op jit(solution)/shard_map/all_to_all | solution.py:43
  515.0 14.2 %all-reduce.6 = (f32[]{:T(128)}, f32[]{:T(128)}) all-reduce(f32[]{:T(128)} %get-tuple-element.135, f32[]{:T(128)} %get-tuple-element.134), channel_id=1, replica_groups=mesh['sector_0'=4,'sector_1'=2,'term_0'=4,'term_1'=4] {'sector_0'}, use_global_device_ids=true, to_apply=%region_30.31 | all-reduce | flops 2 | bytes 16 | tf_op jit(solution)/shard_map/psum | solution.py:16
  529.2 9.4 %all-reduce.9 = (f32[]{:T(128)}, f32[]{:T(128)}) all-reduce(f32[]{:T(128)} %get-tuple-element.200, f32[]{:T(128)} %get-tuple-element.201), channel_id=1, replica_groups=mesh['sector_0'=4,'sector_1'=2,'term_0'=4,'term_1'=4] {'sector_1'}, use_global_device_ids=true, to_apply=%region_31.32 | all-reduce | flops 2 | bytes 16 | tf_op jit(solution)/shard_map/psum | solution.py:16
  538.6 7.4 %all-reduce.3 = (f32[]{:T(128)}, f32[]{:T(128)}) all-reduce(f32[]{:T(128)} %get-tuple-element.206, f32[]{:T(128)} %get-tuple-element.207), channel_id=1, replica_groups=mesh['sector_0'=4,'sector_1'=2,'term_0'=4,'term_1'=4] {'term_0'}, use_global_device_ids=true, to_apply=%region_32.33 | all-reduce | flops 2 | bytes 16 | tf_op jit(solution)/shard_map/psum | solution.py:16
  546.1 7.0 %all-reduce = (f32[]{:T(128)}, f32[]{:T(128)}) all-reduce(f32[]{:T(128)} %get-tuple-element.194, f32[]{:T(128)} %get-tuple-element.195), channel_id=1, replica_groups=mesh['sector_0'=4,'sector_1'=2,'term_0'=4,'term_1'=4] {'term_1'}, use_global_device_ids=true, to_apply=%region_33.34 | all-reduce | flops 2 | bytes 16 | tf_op jit(solution)/shard_map/psum | solution.py:16
  555.1 6.7 %psum.220 = f32[]{:T(128)} all-reduce(f32[]{:T(128)} %get-tuple-element.212), channel_id=1, replica_groups=mesh['sector_0'=4,'sector_1'=2,'term_0'=4,'term_1'=4] {'sector_0'}, use_global_device_ids=true, to_apply=%region_40.41 | all-reduce | flops 1 | bytes 8 | tf_op jit(solution)/shard_map/psum | solution.py:16
  561.8 9.1 %psum.221 = f32[]{:T(128)} all-reduce(f32[]{:T(128)} %psum.220), channel_id=1, replica_groups=mesh['sector_0'=4,'sector_1'=2,'term_0'=4,'term_1'=4] {'sector_1'}, use_global_device_ids=true, to_apply=%region_41.42 | all-reduce | flops 1 | bytes 8 | tf_op jit(solution)/shard_map/psum | solution.py:16
  570.9 7.3 %psum.222 = f32[]{:T(128)} all-reduce(f32[]{:T(128)} %psum.221), channel_id=1, replica_groups=mesh['sector_0'=4,'sector_1'=2,'term_0'=4,'term_1'=4] {'term_0'}, use_global_device_ids=true, to_apply=%region_42.43 | all-reduce | flops 1 | bytes 8 | tf_op jit(solution)/shard_map/psum | solution.py:16
  578.2 7.4 %psum.223 = f32[]{:T(128)} all-reduce(f32[]{:T(128)} %psum.222), channel_id=1, replica_groups=mesh['sector_0'=4,'sector_1'=2,'term_0'=4,'term_1'=4] {'term_1'}, use_global_device_ids=true, to_apply=%region_43.44 | all-reduce | flops 1 | bytes 8 | tf_op jit(solution)/shard_map/psum | solution.py:16
  (43 shorter events, 29.0 us)
Async XLA Ops:
  4.7 36.6 %all-to-all-start = ((f32[16,2,32,512]{3,2,1,0:T(8,128)}), f32[16,2,32,512]{3,2,1,0:T(8,128)S(1)}, u32[]{:S(2)}, u32[]{:S(2)}) async-start(f32[16,2,32,512]{3,2,1,0:T(8,128)} %broadcast_in_dim.23), calls=%async_computation | async-start | bytes 4194304 | tf_op jit(solution)/shard_map/all_to_all | solution.py:21
  42.9 0.7 copy-start.2
  42.9 0.7 copy-start.3
  156.9 0.9 copy-start
  156.9 35.4 %copy-start.1 = (f32[2,32,512]{2,1,0:T(8,128)S(1)}, f32[2,32,512]{2,1,0:T(8,128)}, u32[]{:S(2)}) copy-start(f32[2,32,512]{2,1,0:T(8,128)} %param.15) | copy-start | bytes 393220
  194.0 28.2 %all-to-all-start.2 = ((f32[16,2,32,512]{3,2,1,0:T(8,128)}), f32[16,2,32,512]{3,2,1,0:T(8,128)S(1)}, u32[]{:S(2)}, u32[]{:S(2)}) async-start(f32[16,2,32,512]{3,2,1,0:T(8,128)} %broadcast_in_dim.24), calls=%async_computation.2 | async-start | bytes 4194304 | tf_op jit(solution)/shard_map/all_to_all | solution.py:21
  375.4 28.2 %all-to-all-start.4 = ((f32[16,2,32,512]{3,2,1,0:T(8,128)}), f32[16,2,32,512]{3,2,1,0:T(8,128)S(1)}, u32[]{:S(2)}, u32[]{:S(2)}) async-start(f32[16,2,32,512]{3,2,1,0:T(8,128)} %broadcast_in_dim.25), calls=%async_computation.4 | async-start | bytes 4194304 | tf_op jit(solution)/shard_map/all_to_all | solution.py:21
where the time goes:
time: 595 us; the launch traced here: 588 us
  blocking collectives  431 us (72%)
  waiting for transfers between devices  77 us (13%)
  matrix products  19.4 us (3%)
  starting transfers between devices  16 us (3%)
  local copies, waits for them, and re-layouts  15.7 us (3%)
  loops' own time  15.7 us (3%)
  other arithmetic  7.25 us (1%)
    all_to_all x3, blocking collectives, summed_on_arrival(): tiles = lax.all_to_all(in_blocks(shard, dim, size), axis, 0, 0, tiled=True)  291 us
    psum x16, blocking collectives, over_axes(): return functools.reduce(lax.psum, axes, shard)  140 us
    all_to_all x3, waiting for transfers between devices, from_everyone(): return lax.all_to_all(copies, axis, split_axis=0, concat_axis=0, tiled=True)  77 us
    all_to_all x3, starting transfers between devices, from_everyone(): return lax.all_to_all(copies, axis, split_axis=0, concat_axis=0, tiled=True)  16 us
    another operation x3, loops' own time, apply_tasks(): return lax.fori_loop(first, last, one, partial_value)  15.7 us
  transfers between devices with their start and end apart: 3, of which 3 were waited for; matrix products, arithmetic and copies ran while one was open for 0% of the time, Pallas kernels for 0%

commit v1 on v0

v1 whole, which is shorter than its diff:
```python
import functools

import jax
import jax.numpy as jnp
from jax import lax
from jax.experimental import pallas as pl
from jax.experimental.pallas import tpu as pltpu
from jax.sharding import Mesh
from jax.sharding import PartitionSpec as P

STEPS = 3
LIVE = 7
SECTOR = ("sector_0", "sector_1")
TERM = ("term_0", "term_1")
SECTOR_TERM = SECTOR + TERM
MESH = pl.DeviceIdType.MESH
F32 = jnp.float32
BF16 = jnp.bfloat16


def halves(x):
    hi = x.astype(BF16)
    return hi, (x - hi.astype(F32)).astype(BF16)


def product(a_hi, a_lo, b_hi, b_lo):
    dot = functools.partial(jnp.dot, preferred_element_type=F32)
    return dot(a_hi, b_hi) + dot(a_hi, b_lo) + dot(a_lo, b_hi)


def kernel(
    cells,
    groups,
    trial,
    precond,
    dims,
    source,
    target,
    count,
    left_ops,
    right_ops,
    out,
    ritz,
    vec,
    vec_hi,
    vec_lo,
    part,
    in_f1,
    in_f2,
    in_g1,
    in_g2,
    stage_l,
    stage_r,
    left_hi,
    left_lo,
    right_hi,
    right_lo,
    inner_hi,
    inner_lo,
    own_sums,
    term_sums,
    group_sums,
    sector_sums,
    ag_send,
    ag_recv,
    rs_send,
    f1_recv,
    f2_recv,
    g1_recv,
    g2_recv,
    sum_send,
    sum_recv,
    load_sem,
):
    n_y, n_c = groups
    y, core = lax.axis_index("sector_0"), lax.axis_index("sector_1")
    x, z = lax.axis_index("term_0"), lax.axis_index("term_1")
    slots = left_hi.shape[0]
    width = left_hi.shape[1]
    coords = ((x, z), (z, x))
    names = (("term_0", "term_1"), ("term_1", "term_0"))

    def up(a, by):
        return lax.rem(a + by, 4)

    def unit(c, dp, dq):
        p, q = coords[c]
        return up(p, dp) * 4 + up(q, dq)

    def beside(c, axis, way):
        return {names[c][axis]: up(coords[c][axis], 1 if way == 0 else 3)}

    def load(k, which):
        src, dst = ((right_ops, stage_r), (left_ops, stage_l))[which]
        return pltpu.make_async_copy(src.at[k], dst.at[k], load_sem.at[which, k])

    for which in range(2):
        for k in range(slots):
            load(k, which).start()

    barrier = pltpu.get_barrier_semaphore()
    for d in range(1, 16):
        there = lax.rem(x * 4 + z + d, 16)
        pl.semaphore_signal(
            barrier, inc=1, device_id={"term_0": there // 4, "term_1": lax.rem(there, 4)}, device_id_type=MESH
        )
    n_groups = n_y * n_c
    for d in range(1, n_groups):
        there = lax.rem(y * n_c + core + d, n_groups)
        pl.semaphore_signal(
            barrier, inc=1, device_id={"sector_0": there // n_c, "sector_1": lax.rem(there, n_c)}, device_id_type=MESH
        )

    def mask(c, s):
        row = (x * 4 + z) * 32 + c * 16 + lax.broadcasted_iota(jnp.int32, (16, width), 0)
        col = lax.broadcasted_iota(jnp.int32, (16, width), 1)
        return (row < dims[s]) & (col < dims[s])

    for c in range(2):
        for s in range(2):
            vec[c, unit(c, 0, 0), s] = jnp.where(mask(c, s), trial[s, c * 16 : (c + 1) * 16], 0.0)

    pl.semaphore_wait(barrier, 15 + n_groups - 1)

    def remote(src, dst, send, recv, where):
        return pltpu.make_async_remote_copy(
            src_ref=src, dst_ref=dst, send_sem=send, recv_sem=recv, device_id=where, device_id_type=MESH
        )

    def ag_full(c, line, way, at):
        ref = vec.at[c, at]
        return remote(ref, ref, ag_send, ag_recv.at[c, line, way], beside(c, 0 if line else 1, way))

    def ag_half(c, line, way, at):
        ref = vec.at[c, at, way]
        return remote(ref, ref, ag_send, ag_recv.at[c, line, 2 + way], beside(c, 0 if line else 1, way))

    def lane_sums(value):
        folded = jnp.sum(value.reshape(-1, width), axis=0, keepdims=True)
        total = folded[:, 0:128]
        for i in range(1, width // 128):
            total = total + folded[:, i * 128 : (i + 1) * 128]
        return total

    def squares():
        total = jnp.zeros((1, 128), F32)
        for c in range(2):
            value = vec[c, unit(c, 0, 0)]
            total = total + lane_sums(value * value)
        return total

    def term_start(step):
        for d in range(1, 16):
            there = lax.rem(x * 4 + z + d, 16)
            remote(
                own_sums.at[step],
                term_sums.at[step, x * 4 + z],
                sum_send.at[step, 0],
                sum_recv.at[step, 0],
                {"term_0": there // 4, "term_1": lax.rem(there, 4)},
            ).start()
        term_sums[step, x * 4 + z] = own_sums[step]

    def wait_bytes(ref, sem):
        pltpu.make_async_copy(ref, ref, sem).wait()

    def sector_start(step):
        wait_bytes(term_sums.at[step, 0:15], sum_recv.at[step, 0])
        group_sums[step] = jnp.sum(term_sums[step], axis=0)
        me = y * n_c + core
        for d in range(1, n_groups):
            there = lax.rem(me + d, n_groups)
            remote(
                group_sums.at[step],
                sector_sums.at[step, me],
                sum_send.at[step, 1],
                sum_recv.at[step, 1],
                {"sector_0": there // n_c, "sector_1": lax.rem(there, n_c)},
            ).start()
        sector_sums[step, me] = group_sums[step]

    def sums_end(step):
        if n_groups > 1:
            wait_bytes(sector_sums.at[step, 0 : n_groups - 1], sum_recv.at[step, 1])
        total = jnp.sum(jnp.sum(sector_sums[step], axis=0), axis=1, keepdims=True)
        wait_bytes(term_sums.at[step, 0:15], sum_send.at[step, 0])
        if n_groups > 1:
            wait_bytes(sector_sums.at[step, 0 : n_groups - 1], sum_send.at[step, 1])
        return total

    def prepare(which):
        stage, hi, lo = ((stage_r, right_hi, right_lo), (stage_l, left_hi, left_lo))[which]
        for k in range(slots):
            load(k, which).wait()

        def body(i, carry):
            k = i // 8
            rows = pl.ds(pl.multiple_of(lax.rem(i, 8) * (width // 8), width // 8), width // 8)
            hi[k, rows], lo[k, rows] = halves(stage[k, rows])
            return carry

        lax.fori_loop(0, slots * 8, body, 0)

    def offsets(block):
        px, pz = up(x, block), up(z, block)
        first = [pl.multiple_of(px * 128 + i * 32, 32) for i in range(4)]
        second = [pl.multiple_of(i * 128 + pz * 32 + 16, 16) for i in range(4)]
        return first + second

    def units(c, block):
        return pl.ds(up(coords[c][0], block) * 4, 4)

    def first_products(block):
        for c in range(2):
            for s in range(2):
                vec_hi[s, c, units(c, block)], vec_lo[s, c, units(c, block)] = halves(vec[c, units(c, block), s])
        offs = offsets(block)

        def body(k, carry):
            s = source[k]
            a_hi = jnp.concatenate([vec_hi[s, c, units(c, block)].reshape(64, width) for c in range(2)], axis=0)
            a_lo = jnp.concatenate([vec_lo[s, c, units(c, block)].reshape(64, width) for c in range(2)], axis=0)
            inner = product(a_hi, a_lo, right_hi[k], right_lo[k])
            hi, lo = halves(inner)
            for i, off in enumerate(offs):
                inner_hi[k, pl.ds(off, 16)] = hi[i * 16 : (i + 1) * 16]
                inner_lo[k, pl.ds(off, 16)] = lo[i * 16 : (i + 1) * 16]
            return carry

        lax.fori_loop(0, slots, body, 0)

    def second_products(block):
        offs = offsets(block)
        for c in range(2):
            part[c, units(c, block)] = jnp.zeros((4, 2, 16, width), F32)

        def body(k, carry):
            a_hi = jnp.concatenate([left_hi[k, pl.ds(off, 16)] for off in offs], axis=0)
            a_lo = jnp.concatenate([left_lo[k, pl.ds(off, 16)] for off in offs], axis=0)
            value = product(a_hi, a_lo, inner_hi[k], inner_lo[k])
            live = jnp.where(k < count[0], 1.0, 0.0).astype(F32)
            to_one = live * target[k].astype(F32)
            scale = (live - to_one, to_one)
            for c in range(2):
                piece = value[c * 64 : (c + 1) * 64].reshape(4, 16, width)
                for s in range(2):
                    part[c, units(c, block), s] = part[c, units(c, block), s] + scale[s] * piece
            return carry

        lax.fori_loop(0, slots, body, 0)
        total = jnp.zeros((1, 128), F32)
        for c in range(2):
            for i in range(4):
                at = up(coords[c][0], block) * 4 + i
                total = total + lane_sums(vec[c, at] * part[c, at])
        return total

    def f1(c, dq, way):
        return remote(
            part.at[c, unit(c, 2, dq), way],
            in_f1.at[c, dq, way],
            rs_send,
            f1_recv.at[c, dq, way],
            beside(c, 0, way),
        )

    def f2(c, dq, way):
        return remote(
            part.at[c, unit(c, 1 if way == 0 else 3, dq)],
            in_f2.at[c, dq, way],
            rs_send,
            f2_recv.at[c, dq, way],
            beside(c, 0, way),
        )

    def g1(c, way):
        return remote(
            part.at[c, unit(c, 0, 2), way], in_g1.at[c, way], rs_send, g1_recv.at[c, way], beside(c, 1, way)
        )

    def g2(c, way):
        return remote(
            part.at[c, unit(c, 0, 1 if way == 0 else 3)],
            in_g2.at[c, way],
            rs_send,
            g2_recv.at[c, way],
            beside(c, 1, way),
        )

    def one_step(step, carry):
        for c in range(2):
            for way in range(2):
                ag_full(c, 0, way, unit(c, 0, 0)).start()
        for c in range(2):
            for way in range(2):
                ag_full(c, 1, way, unit(c, 0, 0)).start()

        @pl.when(step == 0)
        def _():
            prepare(0)

        own_sums[step, 1:2] = squares()
        for c in range(2):
            for way in range(2):
                dq = 3 if way == 0 else 1
                at = unit(c, 0, dq)
                ag_full(c, 0, way, at).wait_recv()
                ag_half(c, 0, way, at).start()
                for w in range(2):
                    ag_full(c, 1 + dq, w, at).start()
        for c in range(2):
            for way in range(2):
                at = unit(c, 3 if way == 0 else 1, 0)
                ag_full(c, 1, way, at).wait_recv()
                ag_half(c, 1, way, at).start()
        for c in range(2):
            at = unit(c, 0, 2)
            for way in range(2):
                ag_half(c, 0, way, at).wait_recv()
            for way in range(2):
                ag_full(c, 3, way, at).start()
        first_products(0)

        @pl.when(step == 0)
        def _():
            prepare(1)

        for dq in (1, 3, 2):
            for c in range(2):
                for way in range(2):
                    at = unit(c, 3 if way == 0 else 1, dq)
                    ag_full(c, 1 + dq, way, at).wait_recv()
                    ag_half(c, 1 + dq, way, at).start()
        first_products(1)
        first_products(3)
        for dq in range(4):
            for c in range(2):
                for way in range(2):
                    ag_half(c, 1 + dq, way, unit(c, 2, dq)).wait_recv()
        first_products(2)
        wait_bytes(vec.at[0, 0:15], ag_send)
        wait_bytes(vec.at[1, 0:15], ag_send)

        order = (2, 1, 3, 0)
        total = second_products(2)
        for dq in order:
            for c in range(2):
                for way in range(2):
                    f1(c, dq, way).start()
        total = total + second_products(1)
        total = total + second_products(3)
        for dq in order:
            for c in range(2):
                for way in range(2):
                    f1(c, dq, way).wait_recv()
                    at = unit(c, 1 if way == 0 else 3, dq)
                    part[c, at, way] = part[c, at, way] + in_f1[c, dq, way]
                    f2(c, dq, way).start()
        total = total + second_products(0)
        own_sums[step, 0:1] = total
        term_start(step)

        def take_f2(c, dq):
            at = unit(c, 0, dq)
            for way in range(2):
                f2(c, dq, way).wait_recv()
            part[c, at] = part[c, at] + (in_f2[c, dq, 0] + in_f2[c, dq, 1])

        for c in range(2):
            take_f2(c, 2)
            for way in range(2):
                g1(c, way).start()
        for c in range(2):
            take_f2(c, 1)
            take_f2(c, 3)
        for c in range(2):
            for way in range(2):
                g1(c, way).wait_recv()
                at = unit(c, 0, 1 if way == 0 else 3)
                part[c, at, way] = part[c, at, way] + in_g1[c, way]
                g2(c, way).start()
        sector_start(step)
        for c in range(2):
            take_f2(c, 0)
        for c in range(2):
            for way in range(2):
                g2(c, way).wait_recv()
        sums = sums_end(step)
        vw, vv = sums[0:1], sums[1:2]
        theta = vw / vv
        ritz[step] = theta[0, 0]
        scale = jnp.sqrt(cells / vv)
        for c in range(2):
            at = unit(c, 0, 0)
            for s in range(2):
                w = part[c, at, s] + (in_g2[c, 0, s] + in_g2[c, 1, s])
                w = jnp.where(mask(c, s), w, 0.0)
                v = vec[c, at, s]
                vec[c, at, s] = (v - (w - theta * v) / precond[s, c * 16 : (c + 1) * 16]) * scale
        wait_bytes(part.at[0, 0:15], rs_send)
        wait_bytes(part.at[1, 0:15], rs_send)
        return carry

    lax.fori_loop(0, STEPS, one_step, 0)
    own_sums[STEPS, 0:1] = squares()
    own_sums[STEPS, 1:2] = jnp.zeros((1, 128), F32)
    term_start(STEPS)
    sector_start(STEPS)
    norm = sums_end(STEPS)[0:1]
    scale = jnp.sqrt(cells / norm)
    for c in range(2):
        for s in range(2):
            out[s, c * 16 : (c + 1) * 16] = vec[c, unit(c, 0, 0), s] * scale


def per_device(trial, precond, sector_dims, left_ops, right_ops, task_source, task_target, task_count):
    sec_dev, share, width = trial.shape
    groups = (lax.axis_size("sector_0"), lax.axis_size("sector_1"))
    n_groups = groups[0] * groups[1]
    cells = float(sec_dev * n_groups * width * width)
    vmem = pl.BlockSpec(memory_space=pltpu.VMEM)
    smem = pl.BlockSpec(memory_space=pltpu.SMEM)
    anywhere = pl.BlockSpec(memory_space=pl.ANY)
    dma = pltpu.SemaphoreType.DMA
    ops = (LIVE, width, width)
    return pl.pallas_call(
        functools.partial(kernel, cells, groups),
        out_shape=(
            jax.ShapeDtypeStruct(trial.shape, F32),
            jax.ShapeDtypeStruct((STEPS,), F32),
        ),
        in_specs=[vmem, vmem, smem, smem, smem, smem, anywhere, anywhere],
        out_specs=(vmem, smem),
        scratch_shapes=[
            pltpu.VMEM((2, 16, 2, 16, width), F32),
            pltpu.VMEM((2, 2, 16, 16, width), BF16),
            pltpu.VMEM((2, 2, 16, 16, width), BF16),
            pltpu.VMEM((2, 16, 2, 16, width), F32),
            pltpu.VMEM((2, 4, 2, 16, width), F32),
            pltpu.VMEM((2, 4, 2, 2, 16, width), F32),
            pltpu.VMEM((2, 2, 16, width), F32),
            pltpu.VMEM((2, 2, 2, 16, width), F32),
            pltpu.VMEM(ops, F32),
            pltpu.VMEM(ops, F32),
            pltpu.VMEM(ops, BF16),
            pltpu.VMEM(ops, BF16),
            pltpu.VMEM(ops, BF16),
            pltpu.VMEM(ops, BF16),
            pltpu.VMEM(ops, BF16),
            pltpu.VMEM(ops, BF16),
            pltpu.VMEM((STEPS + 1, 2, 128), F32),
            pltpu.VMEM((STEPS + 1, 16, 2, 128), F32),
            pltpu.VMEM((STEPS + 1, 2, 128), F32),
            pltpu.VMEM((STEPS + 1, n_groups, 2, 128), F32),
            dma,
            dma((2, 5, 4)),
            dma,
            dma((2, 4, 2)),
            dma((2, 4, 2)),
            dma((2, 2)),
            dma((2, 2)),
            dma((STEPS + 1, 2)),
            dma((STEPS + 1, 2)),
            dma((2, LIVE)),
        ],
        compiler_params=pltpu.CompilerParams(
            collective_id=0, has_side_effects=True, vmem_limit_bytes=60 * 1024 * 1024
        ),
    )(trial, precond, sector_dims, task_source, task_target, task_count, left_ops, right_ops)


def solution(mesh):
    finer = Mesh(mesh.devices.reshape(4, 2, 4, 4), SECTOR_TERM)
    placed = (
        P(SECTOR, TERM, None),
        P(SECTOR, TERM, None),
        P(SECTOR),
        P(SECTOR_TERM, None, None),
        P(SECTOR_TERM, None, None),
        P(SECTOR_TERM),
        P(SECTOR_TERM),
        P(SECTOR_TERM),
    )
    return jax.shard_map(
        per_device,
        mesh=finer,
        in_specs=placed,
        out_specs=(P(SECTOR, TERM, None), P()),
        check_vma=False,
    )
```

time: 595 us -> 152 us (0.26); the launches traced: 588 us -> 152 us
  blocking collectives: 431 us -> 0 us
  Pallas kernels: 0 us -> 148 us
  waiting for transfers between devices: 77 us -> 0 us
  matrix products: 19.4 us -> 0 us
  starting transfers between devices: 16 us -> 0 us
  loops' own time: 15.7 us -> 0 us
  local copies, waits for them, and re-layouts: 15.7 us -> 2.74 us
  other arithmetic: 7.25 us -> 0 us
    all_to_all x3 -> x0, blocking collectives: 291 us -> none  [summed_on_arrival(): tiles = lax.all_to_all(in_blocks(shard, dim, size), axis, 0, 0, tiled=True)]
    pallas_call x0 -> x1, Pallas kernels: none -> 148 us  [per_device(): pl.pallas_call(functools.partial(kernel, cells, groups), out_shape=(jax.S...]
    psum x16 -> x0, blocking collectives: 140 us -> none  [over_axes(): return functools.reduce(lax.psum, axes, shard)]
    all_to_all x3 -> x0, waiting for transfers between devices: 77 us -> none  [from_everyone(): return lax.all_to_all(copies, axis, split_axis=0, concat_axis=0, tiled=True)]
    dot_general x6 -> x0, matrix products: 19.4 us -> none  [the longest x3 10.1 us: one(): inner = jnp.dot(block, rights[slot], precision=highest)]
    all_to_all x3 -> x0, starting transfers between devices: 16 us -> none  [from_everyone(): return lax.all_to_all(copies, axis, split_axis=0, concat_axis=0, tiled=True)]
    another operation x3 -> x0, loops' own time: 15.7 us -> none  [apply_tasks(): return lax.fori_loop(first, last, one, partial_value)]
  transfers between devices with their start and end apart: 3 -> 0, of which waited for: 3 -> 0; matrix products, arithmetic and copies ran while one was open for 0% -> 0% of each run, Pallas kernels for 0% -> 0%
where the time goes in v1:
time: 152 us
  Pallas kernels  148 us (97%)
  local copies, waits for them, and re-layouts  2.74 us (2%)
    pallas_call x1, Pallas kernels, per_device(): pl.pallas_call(functools.partial(kernel, cells, groups), out_shape=(jax.S...  148 us

profile of v1, /device:TPU:1, one launch (start us, length us, event | category | flops | bytes accessed | tf_op | source)
XLA Modules:
  0.0 151.6 jit_solution(15343431790848080897)
XLA Ops:
  1.3 147.6 %shard_map.95 = (f32[2,32,512]{2,1,0:T(8,128)}, f32[3]{0:T(128)}) custom-call(f32[2,32,512]{2,1,0:T(8,128)} %trial.1, f32[2,32,512]{2,1,0:T(8,128)} %precond.1, s32[2]{0:T(128)} %dims.1, s32[8]{0:T(128)} %source.1, s32[8]{0:T(128)} %target.1, s32[1]{0:T(128)S(6)} %copy.12.count, f32[8,512,512]{2,1,0:T(8,128)} %left_ops.1, f32[8,512,512]{2,1,0:T(8,128)} %right_ops.1), custom_call_target="tpu_custom_call" | custom-call | tf_op jit(solution)/shard_map/pallas_call | solution.py:426
  148.9 1.6 %copy.13 = f32[2,32,512]{2,1,0:T(8,128)} copy(f32[2,32,512]{2,1,0:T(8,128)} %get-tuple-element.4) | data formatting | bytes 262144
  150.5 1.2 copy.14

commit v2 on v1

v2 whole, which is shorter than its diff:
```python
import functools

import jax
import jax.numpy as jnp
from jax import lax
from jax.experimental import pallas as pl
from jax.experimental.pallas import tpu as pltpu
from jax.sharding import Mesh
from jax.sharding import PartitionSpec as P

STEPS = 3
LIVE = 7
SECTOR = ("sector_0", "sector_1")
TERM = ("term_0", "term_1")
SECTOR_TERM = SECTOR + TERM
MESH = pl.DeviceIdType.MESH
F32 = jnp.float32
BF16 = jnp.bfloat16


def halves(x):
    hi = x.astype(BF16)
    return hi, (x - hi.astype(F32)).astype(BF16)


def product(a_hi, a_lo, b_hi, b_lo):
    dot = functools.partial(jnp.dot, preferred_element_type=F32)
    return dot(a_hi, b_hi) + dot(a_hi, b_lo) + dot(a_lo, b_hi)


def kernel(
    cells,
    groups,
    trial,
    precond,
    dims,
    source,
    target,
    count,
    left_ops,
    right_ops,
    out,
    ritz,
    vec,
    vec_hi,
    vec_lo,
    part,
    in_f1,
    in_fd,
    in_f2,
    in_g,
    base,
    slope,
    last_theta,
    stage_l,
    stage_r,
    left_hi,
    left_lo,
    right_hi,
    right_lo,
    inner_hi,
    inner_lo,
    own_sums,
    term_sums,
    group_sums,
    sector_sums,
    ag_send,
    ag_recv,
    rs_send,
    f1_recv,
    fd_recv,
    f2_recv,
    g_recv,
    sum_send,
    sum_recv,
    load_sem,
):
    n_y, n_c = groups
    y, core = lax.axis_index("sector_0"), lax.axis_index("sector_1")
    x, z = lax.axis_index("term_0"), lax.axis_index("term_1")
    slots = left_hi.shape[0]
    width = left_hi.shape[1]
    coords = ((x, z), (z, x))
    names = (("term_0", "term_1"), ("term_1", "term_0"))

    def up(a, by):
        return lax.rem(a + by, 4)

    def unit(c, dp, dq):
        p, q = coords[c]
        return up(p, dp) * 4 + up(q, dq)

    def beside(c, axis, way):
        return {names[c][axis]: up(coords[c][axis], 1 if way == 0 else 3)}

    def load(k, which):
        src, dst = ((right_ops, stage_r), (left_ops, stage_l))[which]
        return pltpu.make_async_copy(src.at[k], dst.at[k], load_sem.at[which, k])

    for which in range(2):
        for k in range(slots):
            load(k, which).start()

    barrier = pltpu.get_barrier_semaphore()
    for d in range(1, 16):
        there = lax.rem(x * 4 + z + d, 16)
        pl.semaphore_signal(
            barrier, inc=1, device_id={"term_0": there // 4, "term_1": lax.rem(there, 4)}, device_id_type=MESH
        )
    n_groups = n_y * n_c
    for d in range(1, n_groups):
        there = lax.rem(y * n_c + core + d, n_groups)
        pl.semaphore_signal(
            barrier, inc=1, device_id={"sector_0": there // n_c, "sector_1": lax.rem(there, n_c)}, device_id_type=MESH
        )

    def prepare(which):
        stage, hi, lo = ((stage_r, right_hi, right_lo), (stage_l, left_hi, left_lo))[which]
        for k in range(slots):
            load(k, which).wait()

        def body(i, carry):
            k = i // 8
            rows = pl.ds(pl.multiple_of(lax.rem(i, 8) * (width // 8), width // 8), width // 8)
            hi[k, rows], lo[k, rows] = halves(stage[k, rows])
            return carry

        lax.fori_loop(0, slots * 8, body, 0)

    def mask(c, s):
        row = (x * 4 + z) * 32 + c * 16 + lax.broadcasted_iota(jnp.int32, (16, width), 0)
        col = lax.broadcasted_iota(jnp.int32, (16, width), 1)
        return (row < dims[s]) & (col < dims[s])

    for c in range(2):
        for s in range(2):
            vec[c, unit(c, 0, 0), s] = jnp.where(mask(c, s), trial[s, c * 16 : (c + 1) * 16], 0.0)

    pl.semaphore_wait(barrier, 15 + n_groups - 1)

    def remote(src, dst, send, recv, where):
        return pltpu.make_async_remote_copy(
            src_ref=src, dst_ref=dst, send_sem=send, recv_sem=recv, device_id=where, device_id_type=MESH
        )

    def away(c, axis, by):
        return {names[c][axis]: up(coords[c][axis], by)}

    MOVE = (1, 3, 2)

    def ag_row(c, way, at):
        ref = vec.at[c, at]
        return remote(ref, ref, ag_send, ag_recv.at[c, 0, way], away(c, 1, MOVE[way]))

    def ag_full(c, dq, way, at):
        ref = vec.at[c, at]
        return remote(ref, ref, ag_send, ag_recv.at[c, 1 + dq, way], away(c, 0, MOVE[way]))

    def ag_half(c, dq, way, at):
        ref = vec.at[c, at, way]
        return remote(ref, ref, ag_send, ag_recv.at[c, 1 + dq, 2 + way], away(c, 0, MOVE[way]))

    def came(way):
        return (3, 1, 2)[way]

    def lane_sums(value):
        folded = jnp.sum(value.reshape(-1, width), axis=0, keepdims=True)
        total = folded[:, 0:128]
        for i in range(1, width // 128):
            total = total + folded[:, i * 128 : (i + 1) * 128]
        return total

    def squares():
        total = jnp.zeros((1, 128), F32)
        for c in range(2):
            value = vec[c, unit(c, 0, 0)]
            total = total + lane_sums(value * value)
        return total

    def term_start(step):
        for d in range(1, 16):
            there = lax.rem(x * 4 + z + d, 16)
            remote(
                own_sums.at[step],
                term_sums.at[step, x * 4 + z],
                sum_send.at[step, 0],
                sum_recv.at[step, 0],
                {"term_0": there // 4, "term_1": lax.rem(there, 4)},
            ).start()
        term_sums[step, x * 4 + z] = own_sums[step]

    def wait_bytes(ref, sem):
        pltpu.make_async_copy(ref, ref, sem).wait()

    def sector_start(step):
        wait_bytes(term_sums.at[step, 0:15], sum_recv.at[step, 0])
        group_sums[step] = jnp.sum(term_sums[step], axis=0)
        me = y * n_c + core
        for d in range(1, n_groups):
            there = lax.rem(me + d, n_groups)
            remote(
                group_sums.at[step],
                sector_sums.at[step, me],
                sum_send.at[step, 1],
                sum_recv.at[step, 1],
                {"sector_0": there // n_c, "sector_1": lax.rem(there, n_c)},
            ).start()
        sector_sums[step, me] = group_sums[step]

    def sums_end(step):
        if n_groups > 1:
            wait_bytes(sector_sums.at[step, 0 : n_groups - 1], sum_recv.at[step, 1])
        total = jnp.sum(jnp.sum(sector_sums[step], axis=0), axis=1, keepdims=True)
        wait_bytes(term_sums.at[step, 0:15], sum_send.at[step, 0])
        if n_groups > 1:
            wait_bytes(sector_sums.at[step, 0 : n_groups - 1], sum_send.at[step, 1])
        return total

    def spot(c, dp, dq):
        p, q = up(coords[c][0], dp), up(coords[c][1], dq)
        row = (p * 128 + q * 32) if c == 0 else (q * 128 + p * 32 + 16)
        return c, p * 4 + q, pl.multiple_of(row, 16)

    def spots(group):
        return [spot(c, dp, dq) for c in range(2) for dp, dq in group]

    def first_products(group):
        places = spots(group)
        for c, at, _ in places:
            hi, lo = halves(vec[c, at])
            for s in range(2):
                vec_hi[s, c, at], vec_lo[s, c, at] = hi[s], lo[s]

        for k in range(slots):
            s = source[k]
            a_hi = jnp.concatenate([vec_hi[s, c, at] for c, at, _ in places], axis=0)
            a_lo = jnp.concatenate([vec_lo[s, c, at] for c, at, _ in places], axis=0)
            hi, lo = halves(product(a_hi, a_lo, right_hi[k], right_lo[k]))
            for i, (_, _, row) in enumerate(places):
                inner_hi[k, pl.ds(row, 16)] = hi[i * 16 : (i + 1) * 16]
                inner_lo[k, pl.ds(row, 16)] = lo[i * 16 : (i + 1) * 16]

    def second_products(group):
        places = spots(group)
        for k in range(slots):
            a_hi = jnp.concatenate([left_hi[k, pl.ds(row, 16)] for _, _, row in places], axis=0)
            a_lo = jnp.concatenate([left_lo[k, pl.ds(row, 16)] for _, _, row in places], axis=0)
            value = product(a_hi, a_lo, inner_hi[k], inner_lo[k])
            live = jnp.where(k < count[0], 1.0, 0.0).astype(F32)
            to_one = live * target[k].astype(F32)
            scale = (live - to_one, to_one)
            for i, (c, at, _) in enumerate(places):
                piece = value[i * 16 : (i + 1) * 16]
                for s in range(2):
                    old = part[c, at, s] if k else 0.0
                    part[c, at, s] = old + scale[s] * piece
        total = jnp.zeros((1, 128), F32)
        for c, at, _ in places:
            total = total + lane_sums(vec[c, at] * part[c, at])
        return total

    def f1(c, dq, way):
        return remote(
            part.at[c, unit(c, 2, dq), way], in_f1.at[c, dq, way], rs_send, f1_recv.at[c, dq, way], beside(c, 0, way)
        )

    def fd(c):
        return remote(part.at[c, unit(c, 2, 2)], in_fd.at[c], rs_send, fd_recv.at[c], away(c, 0, 2))

    def f2(c, dq, way):
        return remote(
            part.at[c, unit(c, MOVE[way], dq)], in_f2.at[c, dq, way], rs_send, f2_recv.at[c, dq, way], beside(c, 0, way)
        )

    def g(c, way):
        return remote(
            part.at[c, unit(c, 0, MOVE[way])], in_g.at[c, way], rs_send, g_recv.at[c, way], away(c, 1, MOVE[way])
        )

    def one_step(step, carry):
        for c in range(2):
            for way in range(2):
                ag_row(c, way, unit(c, 0, 0)).start()
        for c in range(2):
            for way in range(2):
                ag_full(c, 0, way, unit(c, 0, 0)).start()
        for c in range(2):
            ag_row(c, 2, unit(c, 0, 0)).start()
        @pl.when(step == 0)
        def _():
            prepare(0)

        own_sums[step, 1:2] = squares()
        for c in range(2):
            for way in range(2):
                dq = came(way)
                at = unit(c, 0, dq)
                ag_row(c, way, at).wait_recv()
                for w in range(2):
                    ag_full(c, dq, w, at).start()
        for c in range(2):
            for way in range(2):
                at = unit(c, came(way), 0)
                ag_full(c, 0, way, at).wait_recv()
                ag_half(c, 0, way, at).start()
        for c in range(2):
            at = unit(c, 0, 2)
            ag_row(c, 2, at).wait_recv()
            for w in range(3):
                ag_full(c, 2, w, at).start()
        first_products(((0, 0), (0, 1), (0, 3), (1, 0)))

        @pl.when(step == 0)
        def _():
            prepare(1)

        for dq in (3, 1):
            for c in range(2):
                for way in range(2):
                    at = unit(c, came(way), dq)
                    ag_full(c, dq, way, at).wait_recv()
                    ag_half(c, dq, way, at).start()
        first_products(((3, 0), (0, 2), (1, 1), (1, 3)))
        for c in range(2):
            for way in range(2):
                ag_half(c, 0, way, unit(c, 2, 0)).wait_recv()
                ag_full(c, 2, way, unit(c, came(way), 2)).wait_recv()
        first_products(((3, 1), (3, 3), (2, 0), (1, 2)))
        for c in range(2):
            ag_full(c, 2, 2, unit(c, 2, 2)).wait_recv()
            for dq in (1, 3):
                for way in range(2):
                    ag_half(c, dq, way, unit(c, 2, dq)).wait_recv()
        first_products(((3, 2), (2, 2), (2, 1), (2, 3)))
        wait_bytes(vec.at[0, 0:15], ag_send)
        wait_bytes(vec.at[1, 0:15], ag_send)

        total = second_products(((2, 0), (2, 1), (2, 2), (2, 3)))
        for dq in (1, 3):
            for c in range(2):
                for way in range(2):
                    f1(c, dq, way).start()
        for c in range(2):
            fd(c).start()
        for c in range(2):
            for way in range(2):
                f1(c, 0, way).start()
        total = total + second_products(((1, 2), (3, 2), (1, 1), (3, 1)))
        for c in range(2):
            for way in range(2):
                f2(c, 2, way).start()
        total = total + second_products(((1, 3), (3, 3), (1, 0), (3, 0)))

        def pass_on(c, dq, way):
            f1(c, dq, way).wait_recv()
            at = unit(c, MOVE[way], dq)
            part[c, at, way] = part[c, at, way] + in_f1[c, dq, way]
            f2(c, dq, way).start()

        for dq in (1, 3):
            for c in range(2):
                for way in range(2):
                    pass_on(c, dq, way)
        total = total + second_products(((0, 0), (0, 1), (0, 2), (0, 3)))
        own_sums[step, 0:1] = total
        own_sums[step, 2:3] = jnp.zeros((1, 128), F32)
        term_start(step)

        def take(c, dq):
            at = unit(c, 0, dq)
            for way in range(2):
                f2(c, dq, way).wait_recv()
            extra = in_f2[c, dq, 0] + in_f2[c, dq, 1]
            if dq == 2:
                fd(c).wait_recv()
                extra = extra + in_fd[c]
            part[c, at] = part[c, at] + extra

        for c in range(2):
            take(c, 2)
            g(c, 2).start()
        for c in range(2):
            for way in range(2):
                pass_on(c, 0, way)
        for way in range(2):
            for c in range(2):
                take(c, MOVE[way])
                g(c, way).start()
        sector_start(step)
        for c in range(2):
            take(c, 0)
        for c in range(2):
            for way in range(3):
                g(c, way).wait_recv()
        for c in range(2):
            at = unit(c, 0, 0)
            for s in range(2):
                w = part[c, at, s] + ((in_g[c, 0, s] + in_g[c, 1, s]) + in_g[c, 2, s])
                w = jnp.where(mask(c, s), w, 0.0)
                v = vec[c, at, s]
                p = precond[s, c * 16 : (c + 1) * 16]
                base[c, s] = v - w / p
                slope[c, s] = v / p

        @pl.when(step == STEPS - 1)
        def _():
            a, b = base[...], slope[...]
            own_sums[STEPS, 0:1] = lane_sums(a * a)
            own_sums[STEPS, 1:2] = lane_sums(a * b)
            own_sums[STEPS, 2:3] = lane_sums(b * b)
            term_start(STEPS)

        sums = sums_end(step)
        theta = sums[0:1] / sums[1:2]
        ritz[step] = theta[0, 0]
        scale = jnp.sqrt(cells / sums[1:2])
        for c in range(2):
            vec[c, unit(c, 0, 0)] = (base[c] + theta * slope[c]) * scale
        last_theta[...] = theta
        wait_bytes(part.at[0, 0:15], rs_send)
        wait_bytes(part.at[1, 0:15], rs_send)
        return carry

    lax.fori_loop(0, STEPS, one_step, 0)
    sector_start(STEPS)
    final = sums_end(STEPS)
    theta = last_theta[...]
    norm = final[0:1] + theta * (2.0 * final[1:2] + theta * final[2:3])
    scale = jnp.sqrt(cells / norm)
    for c in range(2):
        for s in range(2):
            out[s, c * 16 : (c + 1) * 16] = (base[c, s] + theta * slope[c, s]) * scale


def handover(vector, quotients, out, ritz):
    out[...] = vector[...]
    for step in range(STEPS):
        ritz[step] = quotients[step]


def per_device(trial, precond, sector_dims, left_ops, right_ops, task_source, task_target, task_count):
    sec_dev, share, width = trial.shape
    groups = (lax.axis_size("sector_0"), lax.axis_size("sector_1"))
    n_groups = groups[0] * groups[1]
    cells = float(sec_dev * n_groups * width * width)
    vmem = pl.BlockSpec(memory_space=pltpu.VMEM)
    smem = pl.BlockSpec(memory_space=pltpu.SMEM)
    anywhere = pl.BlockSpec(memory_space=pl.ANY)
    dma = pltpu.SemaphoreType.DMA
    ops = (LIVE, width, width)
    refined, quotients = pl.pallas_call(
        functools.partial(kernel, cells, groups),
        out_shape=(
            jax.ShapeDtypeStruct(trial.shape, F32),
            jax.ShapeDtypeStruct((STEPS,), F32),
        ),
        in_specs=[vmem, vmem, smem, smem, smem, smem, anywhere, anywhere],
        out_specs=(vmem, smem),
        scratch_shapes=[
            pltpu.VMEM((2, 16, 2, 16, width), F32),
            pltpu.VMEM((2, 2, 16, 16, width), BF16),
            pltpu.VMEM((2, 2, 16, 16, width), BF16),
            pltpu.VMEM((2, 16, 2, 16, width), F32),
            pltpu.VMEM((2, 4, 2, 16, width), F32),
            pltpu.VMEM((2, 2, 16, width), F32),
            pltpu.VMEM((2, 4, 2, 2, 16, width), F32),
            pltpu.VMEM((2, 3, 2, 16, width), F32),
            pltpu.VMEM((2, 2, 16, width), F32),
            pltpu.VMEM((2, 2, 16, width), F32),
            pltpu.VMEM((1, 1), F32),
            pltpu.VMEM(ops, F32),
            pltpu.VMEM(ops, F32),
            pltpu.VMEM(ops, BF16),
            pltpu.VMEM(ops, BF16),
            pltpu.VMEM(ops, BF16),
            pltpu.VMEM(ops, BF16),
            pltpu.VMEM(ops, BF16),
            pltpu.VMEM(ops, BF16),
            pltpu.VMEM((STEPS + 1, 3, 128), F32),
            pltpu.VMEM((STEPS + 1, 16, 3, 128), F32),
            pltpu.VMEM((STEPS + 1, 3, 128), F32),
            pltpu.VMEM((STEPS + 1, n_groups, 3, 128), F32),
            dma,
            dma((2, 5, 4)),
            dma,
            dma((2, 4, 2)),
            dma((2,)),
            dma((2, 4, 2)),
            dma((2, 3)),
            dma((STEPS + 1, 2)),
            dma((STEPS + 1, 2)),
            dma((2, LIVE)),
        ],
        compiler_params=pltpu.CompilerParams(
            collective_id=0, has_side_effects=True, vmem_limit_bytes=60 * 1024 * 1024
        ),
    )(trial, precond, sector_dims, task_source, task_target, task_count, left_ops, right_ops)
    return pl.pallas_call(
        handover,
        out_shape=(jax.ShapeDtypeStruct(trial.shape, F32), jax.ShapeDtypeStruct((STEPS,), F32)),
        in_specs=[vmem, smem],
        out_specs=(vmem, smem),
    )(refined, quotients)


def solution(mesh):
    finer = Mesh(mesh.devices.reshape(4, 2, 4, 4), SECTOR_TERM)
    placed = (
        P(SECTOR, TERM, None),
        P(SECTOR, TERM, None),
        P(SECTOR),
        P(SECTOR_TERM, None, None),
        P(SECTOR_TERM, None, None),
        P(SECTOR_TERM),
        P(SECTOR_TERM),
        P(SECTOR_TERM),
    )
    return jax.shard_map(
        per_device,
        mesh=finer,
        in_specs=placed,
        out_specs=(P(SECTOR, TERM, None), P()),
        check_vma=False,
    )
```

time: 152 us -> 126 us (0.83)
  Pallas kernels: 148 us -> 125 us
  local copies, waits for them, and re-layouts: 2.74 us -> 0 us
    pallas_call x1, Pallas kernels: 148 us -> 123 us  [per_device(): pl.pallas_call(functools.partial(kernel, cells, groups), out_shape=(jax.S...]
    unnamed x2 -> x0, local copies, waits for them, and re-layouts: 2.74 us -> none
    pallas_call x0 -> x1, Pallas kernels: none -> 1.59 us  [per_device(): pl.pallas_call(handover, out_shape=(jax.ShapeDtypeStruct(trial.shape, F32...]
where the time goes in v2:
time: 126 us
  Pallas kernels  125 us (99%)
  between operations  1.29 us (1%)
    pallas_call x1, Pallas kernels, per_device(): pl.pallas_call(functools.partial(kernel, cells, groups), out_shape=(jax.S...  123 us

profile of v2, /device:TPU:1, one launch (start us, length us, event | category | flops | bytes accessed | tf_op | source)
XLA Modules:
  0.0 125.8 jit_solution(5811101277470288472)
XLA Ops:
  1.3 122.9 %shard_map.95 = (f32[2,32,512]{2,1,0:T(8,128)}, f32[3]{0:T(128)}) custom-call(f32[2,32,512]{2,1,0:T(8,128)} %trial.1, f32[2,32,512]{2,1,0:T(8,128)} %precond.1, s32[2]{0:T(128)} %dims.1, s32[8]{0:T(128)} %source.1, s32[8]{0:T(128)} %target.1, s32[1]{0:T(128)S(6)} %copy.10.count, f32[8,512,512]{2,1,0:T(8,128)} %left_ops.1, f32[8,512,512]{2,1,0:T(8,128)} %right_ops.1), custom_call_target="tpu_custom_call" | custom-call | tf_op jit(solution)/shard_map/pallas_call | solution.py:451
  124.2 1.6 %shard_map.96 = (f32[2,32,512]{2,1,0:T(8,128)}, f32[3]{0:T(128)}) custom-call(f32[2,32,512]{2,1,0:T(8,128)} %get-tuple-element.4.vector, f32[3]{0:T(128)} %get-tuple-element.5.quotients), custom_call_target="tpu_custom_call" | custom-call | tf_op jit(solution)/shard_map/pallas_call | solution.py:498

commit v3 on v2

--- a/solution.py
+++ b/solution.py
@@ -62,7 +62,7 @@
     inner_lo,
     own_sums,
     term_sums,
-    group_sums,
+    column_sums,
     sector_sums,
     ag_send,
     ag_recv,
@@ -177,43 +177,44 @@
             total = total + lane_sums(value * value)
         return total
 
-    def term_start(step):
-        for d in range(1, 16):
-            there = lax.rem(x * 4 + z + d, 16)
+    me_sector, me_term = y * n_c + core, x * 4 + z
+
+    def sums_start(step):
+        for d in range(1, n_groups):
+            there = lax.rem(me_sector + d, n_groups)
             remote(
                 own_sums.at[step],
-                term_sums.at[step, x * 4 + z],
+                sector_sums.at[step, me_sector],
                 sum_send.at[step, 0],
                 sum_recv.at[step, 0],
+                {"sector_0": there // n_c, "sector_1": lax.rem(there, n_c)},
+            ).start()
+        sector_sums[step, me_sector] = own_sums[step]
+
+    def wait_bytes(ref, sem):
+        pltpu.make_async_copy(ref, ref, sem).wait()
+
+    def sums_middle(step):
+        if n_groups > 1:
+            wait_bytes(sector_sums.at[step, 0 : n_groups - 1], sum_recv.at[step, 0])
+        column_sums[step] = jnp.sum(sector_sums[step], axis=0)
+        for d in range(1, 16):
+            there = lax.rem(me_term + d, 16)
+            remote(
+                column_sums.at[step],
+                term_sums.at[step, me_term],
+                sum_send.at[step, 1],
+                sum_recv.at[step, 1],
                 {"term_0": there // 4, "term_1": lax.rem(there, 4)},
             ).start()
-        term_sums[step, x * 4 + z] = own_sums[step]
-
-    def wait_bytes(ref, sem):
-        pltpu.make_async_copy(ref, ref, sem).wait()
-
-    def sector_start(step):
-        wait_bytes(term_sums.at[step, 0:15], sum_recv.at[step, 0])
-        group_sums[step] = jnp.sum(term_sums[step], axis=0)
-        me = y * n_c + core
-        for d in range(1, n_groups):
-            there = lax.rem(me + d, n_groups)
-            remote(
-                group_sums.at[step],
-                sector_sums.at[step, me],
-                sum_send.at[step, 1],
-                sum_recv.at[step, 1],
-                {"sector_0": there // n_c, "sector_1": lax.rem(there, n_c)},
-            ).start()
-        sector_sums[step, me] = group_sums[step]
+        term_sums[step, me_term] = column_sums[step]
 
     def sums_end(step):
+        wait_bytes(term_sums.at[step, 0:15], sum_recv.at[step, 1])
+        total = jnp.sum(jnp.sum(term_sums[step], axis=0), axis=1, keepdims=True)
         if n_groups > 1:
-            wait_bytes(sector_sums.at[step, 0 : n_groups - 1], sum_recv.at[step, 1])
-        total = jnp.sum(jnp.sum(sector_sums[step], axis=0), axis=1, keepdims=True)
-        wait_bytes(term_sums.at[step, 0:15], sum_send.at[step, 0])
-        if n_groups > 1:
-            wait_bytes(sector_sums.at[step, 0 : n_groups - 1], sum_send.at[step, 1])
+            wait_bytes(sector_sums.at[step, 0 : n_groups - 1], sum_send.at[step, 0])
+        wait_bytes(term_sums.at[step, 0:15], sum_send.at[step, 1])
         return total
 
     def spot(c, dp, dq):
@@ -364,7 +365,7 @@
         total = total + second_products(((0, 0), (0, 1), (0, 2), (0, 3)))
         own_sums[step, 0:1] = total
         own_sums[step, 2:3] = jnp.zeros((1, 128), F32)
-        term_start(step)
+        sums_start(step)
 
         def take(c, dq):
             at = unit(c, 0, dq)
@@ -382,11 +383,11 @@
         for c in range(2):
             for way in range(2):
                 pass_on(c, 0, way)
+        sums_middle(step)
         for way in range(2):
             for c in range(2):
                 take(c, MOVE[way])
                 g(c, way).start()
-        sector_start(step)
         for c in range(2):
             take(c, 0)
         for c in range(2):
@@ -408,7 +409,7 @@
             own_sums[STEPS, 0:1] = lane_sums(a * a)
             own_sums[STEPS, 1:2] = lane_sums(a * b)
             own_sums[STEPS, 2:3] = lane_sums(b * b)
-            term_start(STEPS)
+            sums_start(STEPS)
 
         sums = sums_end(step)
         theta = sums[0:1] / sums[1:2]
@@ -422,7 +423,7 @@
         return carry
 
     lax.fori_loop(0, STEPS, one_step, 0)
-    sector_start(STEPS)
+    sums_middle(STEPS)
     final = sums_end(STEPS)
     theta = last_theta[...]
     norm = final[0:1] + theta * (2.0 * final[1:2] + theta * final[2:3])

time: 126 us -> 120 us (0.952)
  Pallas kernels: 125 us -> 119 us
    pallas_call x1, Pallas kernels: 123 us -> 117 us  [per_device(): pl.pallas_call(functools.partial(kernel, cells, groups), out_shape=(jax.S...]
where the time goes in v3:
time: 120 us
  Pallas kernels  119 us (99%)
  between operations  1.29 us (1%)
    pallas_call x1, Pallas kernels, per_device(): pl.pallas_call(functools.partial(kernel, cells, groups), out_shape=(jax.S...  117 us

profile of v3, /device:TPU:1, one launch (start us, length us, event | category | flops | bytes accessed | tf_op | source)
XLA Modules:
  0.0 120.4 jit_solution(14194238695624487628)
XLA Ops:
  1.3 117.5 %shard_map.95 = (f32[2,32,512]{2,1,0:T(8,128)}, f32[3]{0:T(128)}) custom-call(f32[2,32,512]{2,1,0:T(8,128)} %trial.1, f32[2,32,512]{2,1,0:T(8,128)} %precond.1, s32[2]{0:T(128)} %dims.1, s32[8]{0:T(128)} %source.1, s32[8]{0:T(128)} %target.1, s32[1]{0:T(128)S(6)} %copy.10.count, f32[8,512,512]{2,1,0:T(8,128)} %left_ops.1, f32[8,512,512]{2,1,0:T(8,128)} %right_ops.1), custom_call_target="tpu_custom_call" | custom-call | tf_op jit(solution)/shard_map/pallas_call | solution.py:452
  118.8 1.6 %shard_map.96 = (f32[2,32,512]{2,1,0:T(8,128)}, f32[3]{0:T(128)}) custom-call(f32[2,32,512]{2,1,0:T(8,128)} %get-tuple-element.4.vector, f32[3]{0:T(128)} %get-tuple-element.5.quotients), custom_call_target="tpu_custom_call" | custom-call | tf_op jit(solution)/shard_map/pallas_call | solution.py:499

commit v4 on v3

--- a/solution.py
+++ b/solution.py
@@ -358,14 +358,14 @@
             part[c, at, way] = part[c, at, way] + in_f1[c, dq, way]
             f2(c, dq, way).start()
 
+        total = total + second_products(((0, 0), (0, 1), (0, 2), (0, 3)))
+        own_sums[step, 0:1] = total
+        own_sums[step, 2:3] = jnp.zeros((1, 128), F32)
+        sums_start(step)
         for dq in (1, 3):
             for c in range(2):
                 for way in range(2):
                     pass_on(c, dq, way)
-        total = total + second_products(((0, 0), (0, 1), (0, 2), (0, 3)))
-        own_sums[step, 0:1] = total
-        own_sums[step, 2:3] = jnp.zeros((1, 128), F32)
-        sums_start(step)
 
         def take(c, dq):
             at = unit(c, 0, dq)

time: 120 us -> 119 us (level)
    pallas_call x1, Pallas kernels: 117 us -> 116 us  [per_device(): pl.pallas_call(functools.partial(kernel, cells, groups), out_shape=(jax.S...]
where the time goes in v4:
time: 119 us
  Pallas kernels  118 us (99%)
  between operations  1.29 us (1%)
    pallas_call x1, Pallas kernels, per_device(): pl.pallas_call(functools.partial(kernel, cells, groups), out_shape=(jax.S...  116 us

profile of v4, /device:TPU:1, one launch (start us, length us, event | category | flops | bytes accessed | tf_op | source)
XLA Modules:
  0.0 118.9 jit_solution(3323974938607479335)
XLA Ops:
  1.3 116.0 %shard_map.95 = (f32[2,32,512]{2,1,0:T(8,128)}, f32[3]{0:T(128)}) custom-call(f32[2,32,512]{2,1,0:T(8,128)} %trial.1, f32[2,32,512]{2,1,0:T(8,128)} %precond.1, s32[2]{0:T(128)} %dims.1, s32[8]{0:T(128)} %source.1, s32[8]{0:T(128)} %target.1, s32[1]{0:T(128)S(6)} %copy.10.count, f32[8,512,512]{2,1,0:T(8,128)} %left_ops.1, f32[8,512,512]{2,1,0:T(8,128)} %right_ops.1), custom_call_target="tpu_custom_call" | custom-call | tf_op jit(solution)/shard_map/pallas_call | solution.py:452
  117.3 1.6 %shard_map.96 = (f32[2,32,512]{2,1,0:T(8,128)}, f32[3]{0:T(128)}) custom-call(f32[2,32,512]{2,1,0:T(8,128)} %get-tuple-element.4.vector, f32[3]{0:T(128)} %get-tuple-element.5.quotients), custom_call_target="tpu_custom_call" | custom-call | tf_op jit(solution)/shard_map/pallas_call | solution.py:499
